TPU v7x, 128 devices: a whole 4x4x4 slice. The times are simulated.
128 devices in a mesh: tok: 8 (over z, core), feat: 16 (over x, y).
Axes of the slice: x: 4, y: 4, z: 4, core: 2. Of those that a mesh axis runs over, the one named last changes fastest.
Arguments:
- residual: bfloat16 [2, 2048, 3584], P(None, 'tok', 'feat'), may hold values from -6 to 6
- enc_weight: bfloat16 [2, 3584, 16384], P(None, None, 'feat'), may hold values from -0.09375 to 0.09375
- enc_bias: float32 [2, 16384], P(None, 'feat'), may hold values from -3 to 3
- dec_sum: bfloat16 [2, 16384, 3584], P(None, 'feat', 'tok'), may hold values from -0.09375 to 0.09375
- unembed: bfloat16 [131072, 3584], P(('tok', 'feat')), may hold values from -6 to 6
- norm_gain: float32 [3584], replicated, may hold values from 0.25 to 1.75
- target_ids: int32 [64], replicated, may hold values from 0 to 131071
- active_ids: int32 [2, 2048, 192], P(None, 'tok', 'feat'), may hold values from -1 to 16383, as said below
Outputs:
- edges: bfloat16 [2, 2048, 12288], P(None, ('tok', 'feat'))
Inputs may be any that keep to these rules, and one draw needn't show every extreme that they name: `active_ids`: slot group g of a token and layer (slots g * 12 to (g + 1) * 12 - 1) holds distinct features of g * 1024 to (g + 1) * 1024 - 1 in its first slots, at least one, and -1 in the rest; in every layer some group is full.
All inputs are finite; a program needn't handle non-finite values.
Results may differ from a plain program's by a relative error of at most 0.0058.
Values may be sent and summed in bfloat16 or wider, within the bound.
No kernel may reach another device: no remote copies, remote signals or barrier semaphores. Data moves between devices by JAX's collectives and lax.ppermute only.
A program may use at most 128 MiB of HBM per device.

v0:
```python
import jax
import jax.numpy as jnp
from jax import lax
from jax.sharding import PartitionSpec as P


def per_device(residual, enc_weight, enc_bias, dec_sum, unembed, norm_gain, target_ids, active_ids):
    n_feat = lax.axis_size("feat")
    feat_pos = lax.axis_index("feat")
    tok_pos = lax.axis_index("tok")
    vocab_rows = unembed.shape[0]
    first_row = (tok_pos * n_feat + feat_pos) * vocab_rows
    selector = (
        target_ids[:, None] - first_row == jnp.arange(vocab_rows, dtype=jnp.int32)[None, :]
    ).astype(jnp.bfloat16)
    partial_rows = jnp.dot(selector, unembed, preferred_element_type=jnp.float32)
    layers = residual.shape[0]
    feat_rows = enc_weight.shape[2]
    width_part = dec_sum.shape[2]
    whole_rows = lax.psum(partial_rows, ("tok", "feat"))
    directions = (whole_rows * norm_gain[None, :]).astype(jnp.bfloat16)
    direction_slice = lax.dynamic_slice_in_dim(directions, tok_pos * width_part, width_part, 1)
    targets = direction_slice.shape[0]
    score_terms = jnp.einsum(
        "lfd,td->lft", dec_sum, direction_slice, preferred_element_type=jnp.float32
    )
    score_terms = score_terms.reshape(layers, feat_rows * targets)
    scores = lax.psum(score_terms, "tok").astype(jnp.bfloat16)
    activations = []
    clamps = []
    for layer_idx in range(layers):
        weights_now = enc_weight[layer_idx]

        def accumulate(running, segment, offset, weights_now=weights_now):
            return jnp.dot(segment, weights_now, preferred_element_type=jnp.float32)

        starting_value = jnp.zeros((residual.shape[1], feat_rows), jnp.float32)
        preactivation = accumulate(
            starting_value,
            lax.all_gather(residual[layer_idx], "feat", axis=1, tiled=True),
            jnp.int32(0),
        )
        preactivation = preactivation + enc_bias[layer_idx][None, :]
        feature_ids = active_ids[layer_idx]
        is_live = feature_ids >= 0
        clipped_activation = jnp.where(is_live, feature_ids - feat_pos * feat_rows, 0)
        values = jnp.take_along_axis(preactivation, clipped_activation, axis=1)
        activations.append(jnp.where(is_live, values, jnp.zeros_like(values)))
        clamps.append(clipped_activation)
    activation = jnp.stack(activations)
    slots = active_ids.shape[2]
    full_table = lax.all_gather(scores, "feat", axis=1, tiled=True).reshape(
        layers, n_feat * feat_rows, targets
    )
    moved_vals = lax.all_to_all(activation, "feat", split_axis=1, concat_axis=2, tiled=True)
    moved_ids = lax.all_to_all(active_ids, "feat", split_axis=1, concat_axis=2, tiled=True)
    live_there = moved_ids >= 0
    clamped_there = jnp.where(live_there, moved_ids, 0)
    blocks = []
    for layer_idx in range(layers):
        picked = jnp.take(full_table[layer_idx], clamped_there[layer_idx], axis=0).astype(
            jnp.float32
        )
        edge_vals = (moved_vals[layer_idx][:, :, None] * picked).astype(jnp.bfloat16)
        blocks.append(edge_vals.reshape(edge_vals.shape[0], n_feat * slots * targets))
    return jnp.stack(blocks)


def solution(mesh):
    return jax.shard_map(
        per_device,
        mesh=mesh,
        in_specs=(
            P(None, "tok", "feat"),
            P(None, None, "feat"),
            P(None, "feat"),
            P(None, "feat", "tok"),
            P(("tok", "feat"), None),
            P(),
            P(),
            P(None, "tok", "feat"),
        ),
        out_specs=P(None, ("tok", "feat"), None),
        check_vma=False,
    )
```

profile of v0, /device:TPU:0, one launch (start us, length us, event | category | flops | bytes accessed | tf_op | source)
XLA Modules:
  0.0 387.2 jit_solution(13353083011878141911)
XLA Ops:
  7.4 0.8 broadcast_subtract_fusion
  8.2 5.5 %fusion.18 = f32[64,3584]{1,0:T(8,128)} fusion(bf16[1024,3584]{1,0:T(8,128)(2,1)} %param.16, s32[64]{0:T(128)S(1)} %broadcast_subtract_fusion), kind=kOutput, calls=%fused_computation.22 | convolution fusion | flops 469827584 | bytes 8257792 | tf_op jit(solution)/shard_map/dot_general | solution.py:16
  13.8 0.7 fusion.33
  15.1 0.8 dynamic-slice
  15.9 149.1 %all-reduce.3.cloned.1.call-done = f32[64,3584]{1,0:T(8,128)} async-done(((f32[64,3584]{1,0:T(8,128)}), f32[64,3584]{1,0:T(8,128)}) %all-reduce.3.cloned.1.call-update) | async-done | bytes 917520 | tf_op jit(solution)/shard_map/psum | solution.py:20
  165.1 1.4 convolution_bitcast_fusion
  166.8 0.5 reshape.38
  167.4 31.5 %all-reduce.4 = bf16[2,65536]{1,0:T(2,128)(2,1)} all-reduce(f32[2,65536]{1,0:T(2,128)S(1)} %reshape.38), channel_id=1, replica_groups=mesh['tok'=8,'feat'=16] {'tok'}, use_global_device_ids=true, to_apply=%region_1.3 | all-reduce | flops 131072 | bytes 786432 | tf_op jit(solution)/shard_map/psum | solution.py:28
  199.1 1.0 reshape.105
  200.1 5.3 %all-to-all-start.1 = ((s32[16,1,384]{2,1,0:T(1,128)}), s32[16,1,384]{2,1,0:T(1,128)S(1)}, u32[]{:S(2)}, u32[]{:S(2)}) async-start(s32[16,1,384]{2,1,0:T(1,128)} %reshape.105), calls=%async_computation.1 | async-start | bytes 49152 | tf_op jit(solution)/shard_map/all_to_all | solution.py:56
  205.9 7.2 %all-to-all-done.1 = s32[16,1,384]{2,1,0:T(1,128)S(1)} async-done(((s32[16,1,384]{2,1,0:T(1,128)}), s32[16,1,384]{2,1,0:T(1,128)S(1)}, u32[]{:S(2)}, u32[]{:S(2)}) %all-to-all-start.1) | async-done | bytes 24608 | tf_op jit(solution)/shard_map/all_to_all | solution.py:56
  213.1 0.6 broadcast.103
  213.7 0.7 reduce.4
  215.4 5.8 %fusion.13 = f32[256,1024]{1,0:T(8,128)S(1)} fusion(bf16[2,3584,1024]{2,1,0:T(8,128)(2,1)} %param.13, bf16[1,256,3584]{1,2,0:T(8,128)(2,1)} %all-gather.10.cloned.1.call-done, f32[1024]{0:T(1024)S(1)} %bitcast.120), kind=kOutput, calls=%fused_computation.17 | convolution fusion | flops 1879310336 | bytes 10227712 | tf_op jit(solution)/shard_map/dot_general | solution.py:35
  221.2 24.7 %gather_fusion.1 = f32[3072]{0:T(1024)S(1)} fusion(f32[256,1024]{1,0:T(8,128)S(1)} %fusion.13, s32[3072]{0:T(1024)S(1)} %reshape.90), kind=kCustom, calls=%fused_computation.2.clone | custom fusion | bytes 49152 | tf_op jit(solution)/shard_map/jit(take_along_axis)/gather | solution.py:47
  246.2 5.7 %fusion.8 = f32[256,1024]{1,0:T(8,128)S(1)} fusion(bf16[2,3584,1024]{2,1,0:T(8,128)(2,1)} %param.13, bf16[1,256,3584]{1,2,0:T(8,128)(2,1)} %all-gather.8.cloned.1.call-done, f32[1024]{0:T(1024)S(1)} %bitcast.119), kind=kOutput, calls=%fused_computation.16 | convolution fusion | flops 1879310336 | bytes 10227712 | tf_op jit(solution)/shard_map/dot_general | solution.py:35
  251.9 24.7 %gather_fusion = f32[3072]{0:T(1024)S(1)} fusion(f32[256,1024]{1,0:T(8,128)S(1)} %fusion.8, s32[3072]{0:T(1024)S(1)} %reshape.85), kind=kCustom, calls=%fused_computation.clone | custom fusion | bytes 49152 | tf_op jit(solution)/shard_map/jit(take_along_axis)/gather | solution.py:47
  277.1 1.0 reshape.107
  278.1 3.7 all-to-all-start
  281.8 7.4 %all-to-all-done = f32[16,1,384]{2,1,0:T(1,128)S(1)} async-done(((f32[16,1,384]{2,1,0:T(1,128)}), f32[16,1,384]{2,1,0:T(1,128)S(1)}, u32[]{:S(2)}, u32[]{:S(2)}) %all-to-all-start) | async-done | bytes 24608 | tf_op jit(solution)/shard_map/all_to_all | solution.py:55
  289.1 0.6 broadcast.104
  289.7 0.7 reduce.5
  291.8 47.4 %slice_reduce_fusion.1 = (bf16[1048576]{0:T(1024)(128)(2,1)}, bf16[1048576]{0:T(1024)(128)(2,1)}) fusion(bf16[2,1048576]{1,0:T(2,128)(2,1)} %all-gather.6.cloned.1.call-done), kind=kLoop, calls=%fused_computation.11 | loop fusion | bytes 8388608 | tf_op jit(solution)/shard_map/slice | solution.py:61
  339.2 6.1 %squeeze.32 = bf16[16384,64]{1,0:T(8,128)(2,1)} reshape(bf16[1048576]{0:T(1024)(128)(2,1)} %get-tuple-element.8) | data formatting | bytes 4194304 | tf_op jit(solution)/shard_map/squeeze | solution.py:61
  345.3 11.0 %gather_fusion.3 = bf16[3072,64]{1,0:T(8,128)(2,1)S(1)} fusion(bf16[16384,64]{1,0:T(8,128)(2,1)} %squeeze.32, s32[3072]{0:T(1024)S(1)} %broadcast_clamp_fusion), kind=kCustom, calls=%fused_computation.3.clone | custom fusion | bytes 798720 | tf_op jit(solution)/shard_map/jit(_take)/gather | solution.py:61
  356.3 1.1 multiply_convert_fusion
  357.4 1.4 stack_reshape.7
  358.8 6.1 %squeeze.30 = bf16[16384,64]{1,0:T(8,128)(2,1)} reshape(bf16[1048576]{0:T(1024)(128)(2,1)} %get-tuple-element.6) | data formatting | bytes 4194304 | tf_op jit(solution)/shard_map/squeeze | solution.py:61
  364.9 11.0 %gather_fusion.2 = bf16[3072,64]{1,0:T(8,128)(2,1)S(1)} fusion(bf16[16384,64]{1,0:T(8,128)(2,1)} %squeeze.30, s32[3072]{0:T(1024)S(1)} %broadcast_clamp_fusion.1), kind=kCustom, calls=%fused_computation.1.clone | custom fusion | bytes 798720 | tf_op jit(solution)/shard_map/jit(_take)/gather | solution.py:61
  375.9 1.1 multiply_convert_fusion.1
  377.0 0.6 stack_reshape.6
  377.6 1.9 pad_maximum_fusion
  (53 shorter events, 4.7 us)
Async XLA Ops:
  7.4 157.7 %copy-start = (bf16[2,1024,448]{1,2,0:T(8,128)(2,1)S(1)}, bf16[2,1024,448]{1,2,0:T(8,128)(2,1)}, u32[]{:S(2)}) copy-start(bf16[2,1024,448]{1,2,0:T(8,128)(2,1)} %param.15) | copy-start | bytes 5505028
  7.4 157.7 %all-reduce.3.cloned.1.call-start = ((), (), s32[]{:S(2)}) async-start(), calls=%async_computation.2 | async-start | bytes 1835008 | tf_op jit(solution)/shard_map/psum | solution.py:20
  8.2 5.6 %copy-start.1 = (bf16[2,256,224]{1,2,0:T(8,128)(2,1)S(1)}, bf16[2,256,224]{1,2,0:T(8,128)(2,1)}, u32[]{:S(2)}) copy-start(bf16[2,256,224]{1,2,0:T(8,128)(2,1)} %param.12) | copy-start | bytes 688132
  13.7 201.7 %all-gather.10.cloned.1.call-start = ((), (), s32[]{:S(2)}) async-start(), calls=%async_computation.5 | async-start | bytes 1949696 | tf_op jit(solution)/shard_map/all_gather | solution.py:40
  14.5 231.7 %all-gather.8.cloned.1.call-start = ((), (), s32[]{:S(2)}) async-start(), calls=%async_computation.4 | async-start | bytes 1949696 | tf_op jit(solution)/shard_map/all_gather | solution.py:40
  15.1 276.7 %all-gather.6.cloned.1.call-start = ((), (), s32[]{:S(2)}) async-start(), calls=%async_computation.3 | async-start | bytes 4456448 | tf_op jit(solution)/shard_map/all_gather | solution.py:52
  166.5 32.4 %copy-start.2 = (s32[2,256,12]{1,0,2:T(2,128)S(1)}, s32[2,256,12]{1,0,2:T(2,128)}, u32[]{:S(2)}) copy-start(s32[2,256,12]{1,0,2:T(2,128)} %param.19) | copy-start | bytes 73732
  166.5 39.0 %copy-start.3 = (f32[2,1024]{1,0:T(2,128)S(1)}, f32[2,1024]{1,0:T(2,128)}, u32[]{:S(2)}) copy-start(f32[2,1024]{1,0:T(2,128)} %param.14) | copy-start | bytes 24580
  200.1 13.1 %all-to-all-start.1 = ((s32[16,1,384]{2,1,0:T(1,128)}), s32[16,1,384]{2,1,0:T(1,128)S(1)}, u32[]{:S(2)}, u32[]{:S(2)}) async-start(s32[16,1,384]{2,1,0:T(1,128)} %reshape.105), calls=%async_computation.1 | async-start | bytes 49152 | tf_op jit(solution)/shard_map/all_to_all | solution.py:56
  278.1 11.0 %all-to-all-start = ((f32[16,1,384]{2,1,0:T(1,128)}), f32[16,1,384]{2,1,0:T(1,128)S(1)}, u32[]{:S(2)}, u32[]{:S(2)}) async-start(f32[16,1,384]{2,1,0:T(1,128)} %reshape.107), calls=%async_computation | async-start | bytes 49152 | tf_op jit(solution)/shard_map/all_to_all | solution.py:55
Sparse Core Ops, SparseCore 0:
  13.8 151.1 all-reduce.2
Sparse Core Ops, SparseCore 1:
  16.4 46.7 all-gather.9
  65.2 43.8 all-gather.7
  199.0 48.3 all-gather.5
where the time goes:
time: 388 us; the launch traced here: 387 us
  waiting for transfers between devices  164 us (42%)
  local copies, waits for them, and re-layouts  142 us (37%)
  blocking collectives  31.5 us (8%)
  matrix products  18.5 us (5%)
  between operations  15.4 us (4%)
  starting transfers between devices  9.12 us (2%)
  other arithmetic  6.43 us (2%)
    psum x1, waiting for transfers between devices, per_device(): whole_rows = lax.psum(partial_rows, ('tok', 'feat'))  149 us
    gather x10, local copies, waits for them, and re-layouts, per_device(): values = jnp.take_along_axis(preactivation, clipped_activation, axis=1)  50.3 us
    slice x1, local copies, waits for them, and re-layouts, per_device(): full_table[layer_idx]  47.4 us
    psum x1, blocking collectives, per_device(): scores = lax.psum(score_terms, 'tok').astype(jnp.bfloat16)  31.5 us
    gather x2, local copies, waits for them, and re-layouts, per_device(): jnp.take(full_table[layer_idx], clamped_there[layer_idx], axis=0)  22.1 us
    squeeze x2, local copies, waits for them, and re-layouts, per_device(): full_table[layer_idx]  12.2 us
    dot_general x2, matrix products, accumulate(): return jnp.dot(segment, weights_now, preferred_element_type=jnp.float32)  11.6 us
  transfers between devices with their start and end apart: 6, of which 3 were waited for; matrix products, arithmetic and copies ran while one was open for 19% of the time, Pallas kernels for 0%

commit v1 on v0

--- a/solution.py
+++ b/solution.py
@@ -25,7 +25,7 @@
         "lfd,td->lft", dec_sum, direction_slice, preferred_element_type=jnp.float32
     )
     score_terms = score_terms.reshape(layers, feat_rows * targets)
-    scores = lax.psum(score_terms, "tok").astype(jnp.bfloat16)
+    scores = jnp.sum(lax.all_gather(score_terms, "tok"), axis=0).astype(jnp.bfloat16)
     activations = []
     clamps = []
     for layer_idx in range(layers):

time: 388 us -> 437 us (1.13)
  waiting for transfers between devices: 164 us -> 239 us
  blocking collectives: 31.5 us -> 0 us
    all_gather x2, waiting for transfers between devices: 0.03 us -> 39.2 us  [per_device(): lax.all_gather(residual[layer_idx], 'feat', axis=1, tiled=True)]
    psum x1 -> x0, blocking collectives: 31.5 us -> none  [per_device(): scores = lax.psum(score_terms, 'tok').astype(jnp.bfloat16)]
    all_gather x0 -> x1, waiting for transfers between devices: none -> 29.6 us  [per_device(): lax.all_gather(score_terms, 'tok')]
    all_gather x1, waiting for transfers between devices: 0.03 us -> 5.65 us  [per_device(): lax.all_gather(scores, 'feat', axis=1, tiled=True)]
    reduce_sum x0 -> x1, other arithmetic: none -> 4.43 us  [per_device(): jnp.sum(lax.all_gather(score_terms, 'tok'), axis=0).astype(jnp.bfloat16)]
  transfers between devices with their start and end apart: 6 -> 7, of which waited for: 3 -> 7; matrix products, arithmetic and copies ran while one was open for 19% -> 17% of each run, Pallas kernels for 0% -> 0%
where the time goes in v1:
time: 437 us; the launch traced here: 436 us
  waiting for transfers between devices  239 us (55%)
  local copies, waits for them, and re-layouts  143 us (33%)
  matrix products  18.3 us (4%)
  between operations  13.4 us (3%)
  starting transfers between devices  11.9 us (3%)
  other arithmetic  10.7 us (2%)
    psum x1, waiting for transfers between devices, per_device(): whole_rows = lax.psum(partial_rows, ('tok', 'feat'))  149 us
    gather x10, local copies, waits for them, and re-layouts, per_device(): values = jnp.take_along_axis(preactivation, clipped_activation, axis=1)  50.3 us
    slice x1, local copies, waits for them, and re-layouts, per_device(): full_table[layer_idx]  47.3 us
    all_gather x2, waiting for transfers between devices, per_device(): lax.all_gather(residual[layer_idx], 'feat', axis=1, tiled=True)  39.2 us
    all_gather x1, waiting for transfers between devices, per_device(): lax.all_gather(score_terms, 'tok')  29.6 us
    gather x2, local copies, waits for them, and re-layouts, per_device(): jnp.take(full_table[layer_idx], clamped_there[layer_idx], axis=0)  22.1 us
    squeeze x2, local copies, waits for them, and re-layouts, per_device(): full_table[layer_idx]  12.2 us
    dot_general x2, matrix products, accumulate(): return jnp.dot(segment, weights_now, preferred_element_type=jnp.float32)  11.5 us
  transfers between devices with their start and end apart: 7, of which 7 were waited for; matrix products, arithmetic and copies ran while one was open for 17% of the time, Pallas kernels for 0%

profile of v1, /device:TPU:0, one launch (start us, length us, event | category | flops | bytes accessed | tf_op | source)
XLA Modules:
  0.0 436.2 jit_solution(6509036408927409486)
XLA Ops:
  6.5 0.8 broadcast_subtract_fusion
  7.3 5.5 %fusion.18 = f32[64,3584]{1,0:T(8,128)} fusion(bf16[1024,3584]{1,0:T(8,128)(2,1)} %param.16, s32[64]{0:T(128)S(1)} %broadcast_subtract_fusion), kind=kOutput, calls=%fused_computation.22 | convolution fusion | flops 469827584 | bytes 8257792 | tf_op jit(solution)/shard_map/dot_general | solution.py:16
  12.9 0.8 dynamic-slice
  13.7 149.2 %all-reduce.2.cloned.1.call-done = f32[64,3584]{1,0:T(8,128)} async-done(((f32[64,3584]{1,0:T(8,128)}), f32[64,3584]{1,0:T(8,128)}) %all-reduce.2.cloned.1.call-update) | async-done | bytes 917520 | tf_op jit(solution)/shard_map/psum | solution.py:20
  162.9 1.4 convolution_bitcast_fusion
  164.6 1.3 all_gather_reshape.3
  166.0 0.7 fusion.33
  167.4 29.6 %all-gather.7.cloned.1.call-done = f32[8,2,65536]{2,1,0:T(2,128)} async-done(((f32[1,2,65536]{2,1,0:T(2,128)}), f32[8,2,65536]{2,1,0:T(2,128)}) %all-gather.7.cloned.1.call-update) | async-done | bytes 4194320 | tf_op jit(solution)/shard_map/all_gather | solution.py:28
  197.0 4.4 %reduce_sum.9 = bf16[2,65536]{1,0:T(2,128)(2,1)} reduce(f32[8,2,65536]{2,1,0:T(2,128)} %all-gather.7.cloned.1.call-done, f32[]{:T(128)} %constant.28.clone.1), dimensions={0}, to_apply=%region_1.3 | reduce | flops 917504 | bytes 4456452 | tf_op jit(solution)/shard_map/reduce_sum | solution.py:28
  201.6 1.0 reshape.101
  202.6 6.8 %all-to-all-start.1 = ((s32[16,1,384]{2,1,0:T(1,128)}), s32[16,1,384]{2,1,0:T(1,128)S(1)}, u32[]{:S(2)}, u32[]{:S(2)}) async-start(s32[16,1,384]{2,1,0:T(1,128)} %reshape.101), calls=%async_computation.1 | async-start | bytes 49152 | tf_op jit(solution)/shard_map/all_to_all | solution.py:56
  210.0 7.1 %all-to-all-done.1 = s32[16,1,384]{2,1,0:T(1,128)S(1)} async-done(((s32[16,1,384]{2,1,0:T(1,128)}), s32[16,1,384]{2,1,0:T(1,128)S(1)}, u32[]{:S(2)}, u32[]{:S(2)}) %all-to-all-start.1) | async-done | bytes 24608 | tf_op jit(solution)/shard_map/all_to_all | solution.py:56
  219.1 24.1 %all-gather.13.cloned.1.call-done = bf16[1,256,3584]{1,2,0:T(8,128)(2,1)} async-done(((bf16[1,256,224]{1,2,0:T(8,128)(2,1)}), bf16[1,256,3584]{1,2,0:T(8,128)(2,1)}) %all-gather.13.cloned.1.call-update) | async-done | bytes 1835024 | tf_op jit(solution)/shard_map/all_gather | solution.py:40
  243.3 5.7 %fusion.13 = f32[256,1024]{1,0:T(8,128)S(1)} fusion(bf16[2,3584,1024]{2,1,0:T(8,128)(2,1)} %param.13, bf16[1,256,3584]{1,2,0:T(8,128)(2,1)} %all-gather.13.cloned.1.call-done, f32[1024]{0:T(1024)S(1)} %bitcast.120), kind=kOutput, calls=%fused_computation.17 | convolution fusion | flops 1879310336 | bytes 10227712 | tf_op jit(solution)/shard_map/dot_general | solution.py:35
  249.0 24.7 %gather_fusion.1 = f32[3072]{0:T(1024)S(1)} fusion(f32[256,1024]{1,0:T(8,128)S(1)} %fusion.13, s32[3072]{0:T(1024)S(1)} %reshape.86), kind=kCustom, calls=%fused_computation.2.clone | custom fusion | bytes 49152 | tf_op jit(solution)/shard_map/jit(take_along_axis)/gather | solution.py:47
  273.9 15.0 %all-gather.11.cloned.1.call-done = bf16[1,256,3584]{1,2,0:T(8,128)(2,1)} async-done(((bf16[1,256,224]{1,2,0:T(8,128)(2,1)}), bf16[1,256,3584]{1,2,0:T(8,128)(2,1)}) %all-gather.11.cloned.1.call-update) | async-done | bytes 1835024 | tf_op jit(solution)/shard_map/all_gather | solution.py:40
  289.0 5.7 %fusion.8 = f32[256,1024]{1,0:T(8,128)S(1)} fusion(bf16[2,3584,1024]{2,1,0:T(8,128)(2,1)} %param.13, bf16[1,256,3584]{1,2,0:T(8,128)(2,1)} %all-gather.11.cloned.1.call-done, f32[1024]{0:T(1024)S(1)} %bitcast.119), kind=kOutput, calls=%fused_computation.16 | convolution fusion | flops 1879310336 | bytes 10227712 | tf_op jit(solution)/shard_map/dot_general | solution.py:35
  294.7 24.7 %gather_fusion = f32[3072]{0:T(1024)S(1)} fusion(f32[256,1024]{1,0:T(8,128)S(1)} %fusion.8, s32[3072]{0:T(1024)S(1)} %reshape.81), kind=kCustom, calls=%fused_computation.clone | custom fusion | bytes 49152 | tf_op jit(solution)/shard_map/jit(take_along_axis)/gather | solution.py:47
  319.9 1.0 reshape.103
  320.9 5.0 %all-to-all-start = ((f32[16,1,384]{2,1,0:T(1,128)}), f32[16,1,384]{2,1,0:T(1,128)S(1)}, u32[]{:S(2)}, u32[]{:S(2)}) async-start(f32[16,1,384]{2,1,0:T(1,128)} %reshape.103), calls=%async_computation | async-start | bytes 49152 | tf_op jit(solution)/shard_map/all_to_all | solution.py:55
  325.8 7.8 %all-to-all-done = f32[16,1,384]{2,1,0:T(1,128)S(1)} async-done(((f32[16,1,384]{2,1,0:T(1,128)}), f32[16,1,384]{2,1,0:T(1,128)S(1)}, u32[]{:S(2)}, u32[]{:S(2)}) %all-to-all-start) | async-done | bytes 24608 | tf_op jit(solution)/shard_map/all_to_all | solution.py:55
  334.2 0.7 reduce.5
  336.3 5.6 %all-gather.9.cloned.1.call-done = bf16[2,1048576]{1,0:T(2,128)(2,1)} async-done(((bf16[2,65536]{1,0:T(2,128)(2,1)}), bf16[2,1048576]{1,0:T(2,128)(2,1)}) %all-gather.9.cloned.1.call-update) | async-done | bytes 4194320 | tf_op jit(solution)/shard_map/all_gather | solution.py:52
  341.9 47.3 %slice_reduce_fusion.1 = (bf16[1048576]{0:T(1024)(128)(2,1)}, bf16[1048576]{0:T(1024)(128)(2,1)}) fusion(bf16[2,1048576]{1,0:T(2,128)(2,1)} %all-gather.9.cloned.1.call-done), kind=kLoop, calls=%fused_computation.11 | loop fusion | bytes 8388608 | tf_op jit(solution)/shard_map/slice | solution.py:61
  389.3 6.1 %squeeze.32 = bf16[16384,64]{1,0:T(8,128)(2,1)} reshape(bf16[1048576]{0:T(1024)(128)(2,1)} %get-tuple-element.8) | data formatting | bytes 4194304 | tf_op jit(solution)/shard_map/squeeze | solution.py:61
  395.4 11.0 %gather_fusion.3 = bf16[3072,64]{1,0:T(8,128)(2,1)S(1)} fusion(bf16[16384,64]{1,0:T(8,128)(2,1)} %squeeze.32, s32[3072]{0:T(1024)S(1)} %broadcast_clamp_fusion), kind=kCustom, calls=%fused_computation.3.clone | custom fusion | bytes 798720 | tf_op jit(solution)/shard_map/jit(_take)/gather | solution.py:61
  406.4 1.1 multiply_convert_fusion
  407.5 1.4 stack_reshape.7
  408.9 6.1 %squeeze.30 = bf16[16384,64]{1,0:T(8,128)(2,1)} reshape(bf16[1048576]{0:T(1024)(128)(2,1)} %get-tuple-element.6) | data formatting | bytes 4194304 | tf_op jit(solution)/shard_map/squeeze | solution.py:61
  414.9 11.0 %gather_fusion.2 = bf16[3072,64]{1,0:T(8,128)(2,1)S(1)} fusion(bf16[16384,64]{1,0:T(8,128)(2,1)} %squeeze.30, s32[3072]{0:T(1024)S(1)} %broadcast_clamp_fusion.1), kind=kCustom, calls=%fused_computation.1.clone | custom fusion | bytes 798720 | tf_op jit(solution)/shard_map/jit(_take)/gather | solution.py:61
  426.0 1.1 multiply_convert_fusion.1
  427.7 1.9 pad_maximum_fusion
  (56 shorter events, 7.0 us)
Async XLA Ops:
  6.5 156.4 %copy-start = (bf16[2,1024,448]{1,2,0:T(8,128)(2,1)S(1)}, bf16[2,1024,448]{1,2,0:T(8,128)(2,1)}, u32[]{:S(2)}) copy-start(bf16[2,1024,448]{1,2,0:T(8,128)(2,1)} %param.15) | copy-start | bytes 5505028
  6.5 156.4 %all-reduce.2.cloned.1.call-start = ((), (), s32[]{:S(2)}) async-start(), calls=%async_computation.2 | async-start | bytes 1835008 | tf_op jit(solution)/shard_map/psum | solution.py:20
  12.8 184.2 %all-gather.7.cloned.1.call-start = ((), (), s32[]{:S(2)}) async-start(), calls=%async_computation.3 | async-start | bytes 4718592 | tf_op jit(solution)/shard_map/all_gather | solution.py:28
  164.6 1.4 copy-start.1
  166.0 77.3 %all-gather.13.cloned.1.call-start = ((), (), s32[]{:S(2)}) async-start(), calls=%async_computation.6 | async-start | bytes 1949696 | tf_op jit(solution)/shard_map/all_gather | solution.py:40
  166.8 122.2 %all-gather.11.cloned.1.call-start = ((), (), s32[]{:S(2)}) async-start(), calls=%async_computation.5 | async-start | bytes 1949696 | tf_op jit(solution)/shard_map/all_gather | solution.py:40
  167.4 34.1 %copy-start.2 = (s32[2,256,12]{1,0,2:T(2,128)S(1)}, s32[2,256,12]{1,0,2:T(2,128)}, u32[]{:S(2)}) copy-start(s32[2,256,12]{1,0,2:T(2,128)} %param.19) | copy-start | bytes 73732
  167.4 42.1 %copy-start.3 = (f32[2,1024]{1,0:T(2,128)S(1)}, f32[2,1024]{1,0:T(2,128)}, u32[]{:S(2)}) copy-start(f32[2,1024]{1,0:T(2,128)} %param.14) | copy-start | bytes 24580
  167.4 174.6 %all-gather.9.cloned.1.call-start = ((), (), s32[]{:S(2)}) async-start(), calls=%async_computation.4 | async-start | bytes 4456448 | tf_op jit(solution)/shard_map/all_gather | solution.py:52
  202.6 14.4 %all-to-all-start.1 = ((s32[16,1,384]{2,1,0:T(1,128)}), s32[16,1,384]{2,1,0:T(1,128)S(1)}, u32[]{:S(2)}, u32[]{:S(2)}) async-start(s32[16,1,384]{2,1,0:T(1,128)} %reshape.101), calls=%async_computation.1 | async-start | bytes 49152 | tf_op jit(solution)/shard_map/all_to_all | solution.py:56
  320.9 12.8 %all-to-all-start = ((f32[16,1,384]{2,1,0:T(1,128)}), f32[16,1,384]{2,1,0:T(1,128)S(1)}, u32[]{:S(2)}, u32[]{:S(2)}) async-start(f32[16,1,384]{2,1,0:T(1,128)} %reshape.103), calls=%async_computation | async-start | bytes 49152 | tf_op jit(solution)/shard_map/all_to_all | solution.py:55
Sparse Core Ops, SparseCore 0:
  12.9 149.8 all-reduce.1
  166.1 30.8 all-gather.6
  199.2 44.0 all-gather.12
  245.3 43.6 all-gather.10
  291.0 50.9 all-gather.8
